TPU v7x, 32 devices: a whole 2x2x4 slice. The times are simulated.
32 devices in a mesh: gx: 4 (over y, core), gy: 4 (over z), frame: 2 (over x).
Axes of the slice: x: 2, y: 2, z: 4, core: 2. Of those that a mesh axis runs over, the one named last changes fastest.
Arguments:
- features: bfloat16 [8, 8, 128, 128], P(('frame', 'gx'), 'gy'), parts along dimension 0, may hold values from -6 to 6
- positions: float32 [8, 8, 3, 128], P(('frame', 'gx'), 'gy'), parts along dimension 0, may hold values from 0 to 1
- bead_types: int32 [8, 8, 128], P(('frame', 'gx'), 'gy'), parts along dimension 0, may hold values from 0 to 15
- cell_counts: int32 [8, 8], P(('frame', 'gx'), 'gy'), parts along dimension 0, may hold values from 48 to 128
- w_value: bfloat16 [128, 128], replicated, may hold values from -0.5 to 0.5
- w_radial: float32 [8, 128], replicated, may hold values from -0.6 to 0.6
- type_gain: float32 [16, 128], replicated, may hold values from 0.1 to 1.9
- w_out: bfloat16 [128, 128], replicated, may hold values from -0.5 to 0.5
- cotangent: bfloat16 [8, 8, 128, 128], P(('frame', 'gx'), 'gy'), parts along dimension 0, may hold values from -6 to 6
Outputs:
- out_feat: bfloat16 [8, 8, 128, 128], P(('frame', 'gx'), 'gy'), parts along dimension 0
- grad_feat: bfloat16 [8, 8, 128, 128], P(('frame', 'gx'), 'gy'), parts along dimension 0
- grad_pos: float32 [8, 8, 3, 128], P(('frame', 'gx'), 'gy'), parts along dimension 0
- grad_wvalue: float32 [256, 128], P('frame'), parts along dimension 0
- grad_wradial: float32 [16, 128], P('frame'), parts along dimension 0
- grad_gain: float32 [32, 128], P('frame'), parts along dimension 0
- grad_wout: float32 [256, 128], P('frame'), parts along dimension 0
There are 2 independent parts, one for each index of `frame`. A program takes and returns all parts, laid end to end along the dimension named above; an argument that names none is the same for every part. Nothing has to cross between parts.
All inputs are finite; a program needn't handle non-finite values.
Results may differ from a plain program's by a relative error of at most 0.012.
Values may be sent and summed in bfloat16 or wider, within the bound.
No kernel may reach another device: no remote copies, remote signals or barrier semaphores. Data moves between devices by JAX's collectives and lax.ppermute only.
A program may use at most 64 MiB of HBM per device.

v0:
```python
import jax
import jax.numpy as jnp
from jax import lax
from jax.sharding import PartitionSpec as P

HZ = 6
soften = 0.01
stencil = [(-1, -1), (-1, 0), (-1, 1), (0, -1), (0, 0), (0, 1), (1, -1), (1, 0), (1, 1)]


def passed_along(block, axis, distance):
    devices = range(lax.axis_size(axis))
    route = [((i - distance) % len(devices), i) for i in devices]
    return lax.ppermute(block, axis, route)


def with_halo(block, sides, width):
    for axis, dim in sides:
        count = lax.axis_size(axis)
        forward = [(i, i + 1) for i in range(count - 1)]
        forward.append((count - 1, 0))
        backward = [(target, source) for source, target in forward]
        low = lax.ppermute(
            lax.slice_in_dim(block, block.shape[dim] - width, None, axis=dim), axis, forward
        )
        high = lax.ppermute(lax.slice_in_dim(block, 0, width, axis=dim), axis, backward)
        block = jnp.concatenate([low, block, high], axis=dim)
    return block


def pair_terms(pos_own, pos_near, shift_x, shift_y, is_self, basis_count):
    slot_count = pos_own.shape[-1]
    offsets = (float(shift_x), float(shift_y), 0.0)
    scales = (1.0, 1.0, float(HZ))
    deltas = [
        (pos_near[:, :, component, None, :] - pos_own[:, :, component, :, None]) * scales[component]
        + offsets[component]
        for component in range(3)
    ]
    dist_sq = deltas[0] * deltas[0] + deltas[1] * deltas[1] + deltas[2] * deltas[2]
    pair_mask = pos_own[:, :, 3, :, None] * pos_near[:, :, 3, None, :]
    if is_self:
        pair_mask = pair_mask * (1.0 - jnp.eye(slot_count, dtype=jnp.float32))
    radius = jnp.sqrt(dist_sq + soften)
    inside = jnp.maximum(1.0 - dist_sq, 0.0)
    envelope = inside * inside
    centres = jnp.arange(basis_count, dtype=jnp.float32) / (basis_count - 1)
    width_gamma = 0.5 * (basis_count - 1) ** 2
    offset_r = radius[:, :, None] - centres[None, None, :, None, None]
    gaussian = jnp.exp(-width_gamma * offset_r * offset_r)
    weights = ((pair_mask * envelope)[:, :, None] * gaussian).astype(jnp.bfloat16)
    slope_r2 = (
        pair_mask[:, :, None]
        * gaussian
        * (
            -2.0 * inside[:, :, None]
            - envelope[:, :, None] * width_gamma * offset_r / radius[:, :, None]
        )
    )
    scaled_deltas = [deltas[component] * scales[component] for component in range(3)]
    return (weights, slope_r2, scaled_deltas)


def fold_back(pos_accum, val_accum):
    row_count = pos_accum.shape[0] - 2
    for step_by, source, target in ((1, row_count + 1, 1), (-1, 0, row_count)):
        received = passed_along((pos_accum[source], val_accum[source]), "gx", step_by)
        pos_accum = pos_accum.at[target].add(received[0])
        val_accum = val_accum.at[target].add(received[1])
    pos_accum = pos_accum[1 : row_count + 1]
    val_accum = val_accum[1 : row_count + 1]
    col_count = pos_accum.shape[1] - 2
    for step_by, source, target in ((1, col_count + 1, 1), (-1, 0, col_count)):
        received = passed_along((pos_accum[:, source], val_accum[:, source]), "gy", step_by)
        pos_accum = pos_accum.at[:, target].add(received[0])
        val_accum = val_accum.at[:, target].add(received[1])
    return (pos_accum[:, 1 : col_count + 1], val_accum[:, 1 : col_count + 1])


def on_device(
    features, positions, bead_types, cell_counts, w_value, w_radial, type_gain, w_out, cotangent
):
    row_count, col_count, slot_count, channels = features.shape
    basis_count = w_radial.shape[0]
    valid_slot = (
        jnp.arange(slot_count, dtype=jnp.int32)[None, None, :] < cell_counts[:, :, None]
    ).astype(jnp.float32)
    pos_valid = jnp.concatenate([positions, valid_slot[:, :, None, :]], axis=2)
    flat_feat = features.reshape(-1, channels)
    projected = jnp.dot(flat_feat, w_value, preferred_element_type=jnp.float32)
    onehot = (
        bead_types.reshape(-1)[:, None] == jnp.arange(type_gain.shape[0], dtype=jnp.int32)[None, :]
    ).astype(jnp.float32)
    bead_gain = jnp.dot(onehot, type_gain, precision=lax.Precision.HIGHEST)
    carried = (
        (projected * bead_gain)
        .astype(jnp.bfloat16)
        .reshape(row_count, col_count, slot_count, channels)
    )
    pos_ext = with_halo(pos_valid, (("gx", 0), ("gy", 1)), 1)
    val_ext = with_halo(carried, (("gx", 0), ("gy", 1)), 1)

    def near_cells(extended, shift_x, shift_y):
        return extended[
            1 + shift_x : 1 + shift_x + row_count, 1 + shift_y : 1 + shift_y + col_count
        ]

    summed = jnp.zeros((row_count, col_count, basis_count, slot_count, channels), jnp.float32)
    for shift_x, shift_y in stencil:
        weights, slope_r2, deltas = pair_terms(
            pos_valid,
            near_cells(pos_ext, shift_x, shift_y),
            shift_x,
            shift_y,
            shift_x == 0 and shift_y == 0,
            basis_count,
        )
        summed = summed + jnp.einsum(
            "abkij,abjc->abkic",
            weights,
            near_cells(val_ext, shift_x, shift_y),
            preferred_element_type=jnp.float32,
        )
    aggregate = jnp.sum(summed * w_radial[None, None, :, None, :], axis=2)
    agg_half = aggregate.astype(jnp.bfloat16).reshape(-1, channels)
    pre_act = jnp.dot(agg_half, w_out, preferred_element_type=jnp.float32)
    sigmoid_act = jax.nn.sigmoid(pre_act)
    out_feat = (flat_feat.astype(jnp.float32) + pre_act * sigmoid_act).astype(jnp.bfloat16)
    grad_pre = (
        cotangent.reshape(-1, channels).astype(jnp.float32)
        * sigmoid_act
        * (1.0 + pre_act * (1.0 - sigmoid_act))
    ).astype(jnp.bfloat16)
    grad_wout = jnp.dot(agg_half.T, grad_pre, preferred_element_type=jnp.float32)
    grad_agg = (
        jnp.dot(grad_pre, w_out.T, preferred_element_type=jnp.float32)
        .astype(jnp.bfloat16)
        .reshape(row_count, col_count, slot_count, channels)
    )
    grad_wradial = jnp.sum(summed * grad_agg.astype(jnp.float32)[:, :, None], axis=(0, 1, 3))
    scaled = (grad_agg.astype(jnp.float32)[:, :, None] * w_radial[None, None, :, None, :]).astype(
        jnp.bfloat16
    )
    pos_accum = jnp.zeros((row_count + 2, col_count + 2, 3, slot_count), jnp.float32)
    val_accum = jnp.zeros((row_count + 2, col_count + 2, slot_count, channels), jnp.float32)
    for shift_x, shift_y in stencil:
        weights, slope_r2, deltas = pair_terms(
            pos_valid,
            near_cells(pos_ext, shift_x, shift_y),
            shift_x,
            shift_y,
            shift_x == 0 and shift_y == 0,
            basis_count,
        )
        weight_grad = jnp.einsum(
            "abkic,abjc->abkij",
            scaled,
            near_cells(val_ext, shift_x, shift_y),
            preferred_element_type=jnp.float32,
        )
        pair_pull = jnp.sum(weight_grad * slope_r2, axis=2)
        own_pull = jnp.stack(
            [-2.0 * jnp.sum(pair_pull * delta_one, axis=3) for delta_one in deltas], axis=2
        )
        far_pull = jnp.stack(
            [2.0 * jnp.sum(pair_pull * delta_one, axis=2) for delta_one in deltas], axis=2
        )
        far_value = jnp.einsum(
            "abkij,abkic->abjc", weights, scaled, preferred_element_type=jnp.float32
        )
        pos_accum = pos_accum.at[1 : row_count + 1, 1 : col_count + 1].add(own_pull)
        pos_accum = pos_accum.at[
            1 + shift_x : 1 + shift_x + row_count, 1 + shift_y : 1 + shift_y + col_count
        ].add(far_pull)
        val_accum = val_accum.at[
            1 + shift_x : 1 + shift_x + row_count, 1 + shift_y : 1 + shift_y + col_count
        ].add(far_value)
    grad_pos, grad_carried = fold_back(pos_accum, val_accum)
    flat_carried = grad_carried.reshape(-1, channels)
    grad_half = (flat_carried * bead_gain).astype(jnp.bfloat16)
    grad_feat = (
        cotangent.reshape(-1, channels).astype(jnp.float32)
        + jnp.dot(grad_half, w_value.T, preferred_element_type=jnp.float32)
    ).astype(jnp.bfloat16)
    grad_wvalue = jnp.dot(flat_feat.T, grad_half, preferred_element_type=jnp.float32)
    grad_gain = jnp.dot(onehot.T, flat_carried * projected, precision=lax.Precision.HIGHEST)
    summed_grads = lax.psum((grad_wvalue, grad_wradial, grad_gain, grad_wout), ("gx", "gy"))
    return (
        out_feat.reshape(row_count, col_count, slot_count, channels),
        grad_feat.reshape(row_count, col_count, slot_count, channels),
        grad_pos,
        summed_grads[0],
        summed_grads[1],
        summed_grads[2],
        summed_grads[3],
    )


def solution(mesh):
    return jax.shard_map(
        on_device,
        mesh=mesh,
        in_specs=(
            P(("frame", "gx"), "gy", None, None),
            P(("frame", "gx"), "gy", None, None),
            P(("frame", "gx"), "gy", None),
            P(("frame", "gx"), "gy"),
            P(),
            P(),
            P(),
            P(),
            P(("frame", "gx"), "gy", None, None),
        ),
        out_specs=(
            P(("frame", "gx"), "gy", None, None),
            P(("frame", "gx"), "gy", None, None),
            P(("frame", "gx"), "gy", None, None),
            P("frame", None),
            P("frame", None),
            P("frame", None),
            P("frame", None),
        ),
        check_vma=False,
    )
```

profile of v0, /device:TPU:8, one launch (start us, length us, event | category | flops | bytes accessed | tf_op | source)
XLA Modules:
  0.0 182.1 jit_solution(11763310224023146852)
XLA Ops:
  8.0 1.7 collective-permute-start.1
  10.8 1.7 collective-permute-start.4
  14.6 1.6 collective-permute-start.2
  16.7 1.6 collective-permute-done.2
  18.4 1.5 collective-permute-done.6
  21.9 1.6 collective-permute-start.5
  24.8 2.5 %collective-permute-done.5 = bf16[3,1,128,128]{3,2,1,0:T(8,128)(2,1)S(1)} collective-permute-done((bf16[3,1,128,128]{3,2,1,0:T(8,128)(2,1)S(1)}, bf16[3,1,128,128]{3,2,1,0:T(8,128)(2,1)S(1)}, u32[]{:S(2)}, u32[]{:S(2)}) %collective-permute-start.5) | collective-permute-done | bytes 98336 | tf_op jit(solution)/shard_map/ppermute | solution.py:23
  33.9 1.8 %fusion.16 = f32[3,4,128,128]{3,2,1,0:T(8,128)S(1)} fusion(f32[3,4,128,128]{3,2,1,0:T(8,128)S(1)} %scatter-add.104, s32[]{:T(128)} %bitcast.74, s32[]{:T(128)} %bitcast.75, f32[2,128,128]{2,1,0:T(8,128)S(1)} %bitcast_convert_fusion, f32[8,128]{1,0:T(8,128)S(1)} %copy-done.9, f32[2,128,128]{2,1,0:T(8,128)S(1)} %get-tuple-element.666, ...), kind=kOutput, calls=%fused_computation.63 | convolution fusion | flops 68976640 | bytes 659976 | tf_op jit(solution)/shard_map/abkij,abkic->abjc/dot_general | solution.py:168
  35.8 2.5 %fusion.19 = f32[3,4,128,128]{3,2,1,0:T(8,128)S(1)} fusion(f32[3,4,128,128]{3,2,1,0:T(8,128)S(1)} %fusion.16, s32[]{:T(128)} %bitcast.79, s32[]{:T(128)} %bitcast.80, f32[2,128,128]{2,1,0:T(8,128)S(1)} %bitcast_convert_fusion, f32[8,128]{1,0:T(8,128)S(1)} %copy-done.9, f32[2,128,128]{2,1,0:T(8,128)S(1)} %get-tuple-element.653, ...), kind=kOutput, calls=%fused_computation.66 | convolution fusion | flops 69009408 | bytes 659977 | tf_op jit(solution)/shard_map/abkij,abkic->abjc/dot_general | solution.py:168
  49.5 1.3 fusion.280
  50.8 1.4 scatter-add.126
  52.4 2.0 %add_select_fusion = f32[1,2,3,128]{3,1,2,0:T(2,128)S(1)} fusion(f32[3,4,3,128]{3,1,2,0:T(4,128)S(1)} %scatter-add.129, s32[]{:T(128)} %bitcast.79, s32[]{:T(128)} %bitcast.80, f32[1,2,1,128]{3,1,2,0:T(2,128)S(1)} %get-tuple-element.726, f32[1,2,1,128]{3,1,2,0:T(2,128)S(1)} %get-tuple-element.727, f32[1,2,1,128]{3,1,2,0:T(2,128)S(1)} %get-tuple-element.728, ...), kind=kLoop, calls=%fused_computation.451 | loop fusion | flops 3072 | bytes 9225 | tf_op jit(solution)/shard_map/select.53
  54.4 1.4 scatter-add.130
  57.3 1.7 collective-permute-start.13
  59.9 1.7 collective-permute-start.9
  63.0 2.3 %collective-permute-done.14 = f32[1,3,128]{2,0,1:T(1,128)S(1)} collective-permute-done((f32[1,3,128]{2,0,1:T(1,128)S(1)}, f32[1,3,128]{2,0,1:T(1,128)S(1)}, u32[]{:S(2)}, u32[]{:S(2)}) %collective-permute-start.14) | collective-permute-done | bytes 1568 | tf_op jit(solution)/shard_map/ppermute | solution.py:14
  65.3 1.5 collective-permute-done.8
  67.4 1.5 collective-permute-start.10
  69.5 2.9 %collective-permute-done.10 = f32[1,128,128]{2,1,0:T(8,128)S(1)} collective-permute-done((f32[1,128,128]{2,1,0:T(8,128)S(1)}, f32[1,128,128]{2,1,0:T(8,128)S(1)}, u32[]{:S(2)}, u32[]{:S(2)}) %collective-permute-start.10) | collective-permute-done | bytes 65568 | tf_op jit(solution)/shard_map/ppermute | solution.py:14
  72.5 2.7 %collective-permute-start.11 = (f32[1,128,128]{2,1,0:T(8,128)S(1)}, f32[1,128,128]{2,1,0:T(8,128)S(1)}, u32[]{:S(2)}, u32[]{:S(2)}) collective-permute-start(f32[1,128,128]{2,1,0:T(8,128)S(1)} %slice_bitcast_fusion.2), channel_id=1, source_target_pairs={{2,0},{4,2},{6,4},{0,6},{3,1},{5,3},{7,5},{1,7},{10,8},{12,10},{14... | collective-permute-start | bytes 196616 | tf_op jit(solution)/shard_map/ppermute | solution.py:14
  75.8 1.3 collective-permute-done.11
  79.1 58.6 %all-reduce.2 = (f32[8,128]{1,0:T(8,128)}, f32[16,128]{1,0:T(8,128)}) all-reduce(f32[8,128]{1,0:T(8,128)S(1)} %multiply_reduce_fusion, f32[16,128]{1,0:T(8,128)S(1)} %fusion.203), channel_id=1, replica_groups=mesh['gx'=4,'gy'=4,'frame'=2] {'gx','gy'}, use_global_device_ids=true, to_apply=%region_67.0 | all-reduce | flops 3072 | bytes 24576 | tf_op jit(solution)/shard_map/psum | solution.py:187
  137.7 35.2 %all-reduce.6.cloned.1.call-done = (f32[128,128]{0,1:T(8,128)}, f32[128,128]{1,0:T(8,128)}) async-done(((f32[128,128]{0,1:T(8,128)}, f32[128,128]{1,0:T(8,128)}), (f32[128,128]{0,1:T(8,128)}, f32[128,128]{1,0:T(8,128)})) %all-reduce.6.cloned.1.call-update) | async-done | bytes 131088 | tf_op jit(solution)/shard_map/psum | solution.py:187
  173.0 1.6 copy.44
  (179 shorter events, 33.2 us)
Async XLA Ops:
  7.2 24.9 %copy-start = (bf16[128,128]{1,0:T(8,128)(2,1)S(1)}, bf16[128,128]{1,0:T(8,128)(2,1)}, u32[]{:S(2)}) copy-start(bf16[128,128]{1,0:T(8,128)(2,1)} %param.86) | copy-start | bytes 98308
  7.2 2.5 %copy-start.8 = (f32[16,128]{1,0:T(8,128)S(1)}, f32[16,128]{1,0:T(8,128)}, u32[]{:S(2)}) copy-start(f32[16,128]{1,0:T(8,128)} %param.85) | copy-start | bytes 24580
  7.2 165.8 %all-reduce.6.cloned.1.call-start = ((), (), s32[]{:S(2)}) async-start(), calls=%async_computation | async-start | bytes 262144 | tf_op jit(solution)/shard_map/psum | solution.py:187
  7.9 1.8 copy-start.10
  7.9 6.7 %collective-permute-start = (f32[1,2,4,128]{3,1,2,0:T(2,128)S(1)}, f32[1,2,4,128]{3,1,2,0:T(2,128)S(1)}, u32[]{:S(2)}, u32[]{:S(2)}) collective-permute-start(f32[1,2,4,128]{3,1,2,0:T(2,128)S(1)} %pad_maximum_fusion.8), channel_id=1, source_target_pairs={{0,8},{8,16},{16,24},{24,0},{1,9},{9,17},{17,25},{25,1},{2,10},{10... | collective-permute-start | bytes 12296 | tf_op jit(solution)/shard_map/ppermute | solution.py:23
  8.0 6.6 %collective-permute-start.1 = (f32[1,2,4,128]{3,1,2,0:T(2,128)S(1)}, f32[1,2,4,128]{3,1,2,0:T(2,128)S(1)}, u32[]{:S(2)}, u32[]{:S(2)}) collective-permute-start(f32[1,2,4,128]{3,1,2,0:T(2,128)S(1)} %pad_maximum_fusion.8), channel_id=1, source_target_pairs={{8,0},{16,8},{24,16},{0,24},{9,1},{17,9},{25,17},{1,25},{10,2},{18... | collective-permute-start | bytes 12296 | tf_op jit(solution)/shard_map/ppermute | solution.py:26
  9.7 0.8 copy-start.3
  10.7 11.1 %collective-permute-start.3 = (bf16[1,2,128,128]{3,2,1,0:T(8,128)(2,1)S(1)}, bf16[1,2,128,128]{3,2,1,0:T(8,128)(2,1)S(1)}, u32[]{:S(2)}, u32[]{:S(2)}) collective-permute-start(bf16[1,2,128,128]{3,2,1,0:T(8,128)(2,1)S(1)} %bitcast.388), channel_id=1, source_target_pairs={{0,8},{8,16},{16,24},{24,0},{1,9},{9,17},{17,25},{25,1},{2,10},{10... | collective-permute-start | bytes 196616 | tf_op jit(solution)/shard_map/ppermute | solution.py:23
  10.8 11.0 %collective-permute-start.4 = (bf16[1,2,128,128]{3,2,1,0:T(8,128)(2,1)S(1)}, bf16[1,2,128,128]{3,2,1,0:T(8,128)(2,1)S(1)}, u32[]{:S(2)}, u32[]{:S(2)}) collective-permute-start(bf16[1,2,128,128]{3,2,1,0:T(8,128)(2,1)S(1)} %bitcast.389), channel_id=1, source_target_pairs={{8,0},{16,8},{24,16},{0,24},{9,1},{17,9},{25,17},{1,25},{10,2},{18... | collective-permute-start | bytes 196616 | tf_op jit(solution)/shard_map/ppermute | solution.py:26
  14.6 3.7 %collective-permute-start.2 = (f32[3,1,4,128]{3,1,2,0:T(1,128)S(1)}, f32[3,1,4,128]{3,1,2,0:T(1,128)S(1)}, u32[]{:S(2)}, u32[]{:S(2)}) collective-permute-start(f32[3,1,4,128]{3,1,2,0:T(1,128)S(1)} %get-tuple-element.616), channel_id=1, source_target_pairs={{0,2},{2,4},{4,6},{6,0},{1,3},{3,5},{5,7},{7,1},{8,10},{10,12},{12... | collective-permute-start | bytes 18440 | tf_op jit(solution)/shard_map/ppermute | solution.py:23
  16.3 3.6 %collective-permute-start.6 = (f32[3,1,4,128]{3,1,2,0:T(1,128)S(1)}, f32[3,1,4,128]{3,1,2,0:T(1,128)S(1)}, u32[]{:S(2)}, u32[]{:S(2)}) collective-permute-start(f32[3,1,4,128]{3,1,2,0:T(1,128)S(1)} %get-tuple-element.617), channel_id=1, source_target_pairs={{2,0},{4,2},{6,4},{0,6},{3,1},{5,3},{7,5},{1,7},{10,8},{12,10},{14... | collective-permute-start | bytes 18440 | tf_op jit(solution)/shard_map/ppermute | solution.py:26
  21.9 5.4 %collective-permute-start.5 = (bf16[3,1,128,128]{3,2,1,0:T(8,128)(2,1)S(1)}, bf16[3,1,128,128]{3,2,1,0:T(8,128)(2,1)S(1)}, u32[]{:S(2)}, u32[]{:S(2)}) collective-permute-start(bf16[3,1,128,128]{3,2,1,0:T(8,128)(2,1)S(1)} %get-tuple-element.582), channel_id=1, source_target_pairs={{0,2},{2,4},{4,6},{6,0},{1,3},{3,5},{5,7},{7,1},{8,10},{10,12},{12... | collective-permute-start | bytes 294920 | tf_op jit(solution)/shard_map/ppermute | solution.py:23
  23.5 5.3 %collective-permute-start.7 = (bf16[3,1,128,128]{3,2,1,0:T(8,128)(2,1)S(1)}, bf16[3,1,128,128]{3,2,1,0:T(8,128)(2,1)S(1)}, u32[]{:S(2)}, u32[]{:S(2)}) collective-permute-start(bf16[3,1,128,128]{3,2,1,0:T(8,128)(2,1)S(1)} %get-tuple-element.583), channel_id=1, source_target_pairs={{2,0},{4,2},{6,4},{0,6},{3,1},{5,3},{7,5},{1,7},{10,8},{12,10},{14... | collective-permute-start | bytes 294920 | tf_op jit(solution)/shard_map/ppermute | solution.py:26
  57.3 4.4 %collective-permute-start.12 = (f32[4,3,128]{2,0,1:T(4,128)S(1)}, f32[4,3,128]{2,0,1:T(4,128)S(1)}, u32[]{:S(2)}, u32[]{:S(2)}) collective-permute-start(f32[4,3,128]{2,0,1:T(4,128)S(1)} %get-tuple-element.590), channel_id=1, source_target_pairs={{24,0},{0,8},{8,16},{16,24},{25,1},{1,9},{9,17},{17,25},{26,2},{2,... | collective-permute-start | bytes 18440 | tf_op jit(solution)/shard_map/ppermute | solution.py:14
  57.3 4.3 %collective-permute-start.13 = (f32[4,3,128]{2,0,1:T(4,128)S(1)}, f32[4,3,128]{2,0,1:T(4,128)S(1)}, u32[]{:S(2)}, u32[]{:S(2)}) collective-permute-start(f32[4,3,128]{2,0,1:T(4,128)S(1)} %get-tuple-element.591), channel_id=1, source_target_pairs={{8,0},{16,8},{24,16},{0,24},{9,1},{17,9},{25,17},{1,25},{10,2},{18... | collective-permute-start | bytes 18440 | tf_op jit(solution)/shard_map/ppermute | solution.py:14
  59.9 6.9 %collective-permute-start.8 = (f32[4,128,128]{2,1,0:T(8,128)S(1)}, f32[4,128,128]{2,1,0:T(8,128)S(1)}, u32[]{:S(2)}, u32[]{:S(2)}) collective-permute-start(f32[4,128,128]{2,1,0:T(8,128)S(1)} %get-tuple-element.574), channel_id=1, source_target_pairs={{24,0},{0,8},{8,16},{16,24},{25,1},{1,9},{9,17},{17,25},{26,2},{2,... | collective-permute-start | bytes 786440 | tf_op jit(solution)/shard_map/ppermute | solution.py:14
  59.9 7.5 %collective-permute-start.9 = (f32[4,128,128]{2,1,0:T(8,128)S(1)}, f32[4,128,128]{2,1,0:T(8,128)S(1)}, u32[]{:S(2)}, u32[]{:S(2)}) collective-permute-start(f32[4,128,128]{2,1,0:T(8,128)S(1)} %get-tuple-element.575), channel_id=1, source_target_pairs={{8,0},{16,8},{24,16},{0,24},{9,1},{17,9},{25,17},{1,25},{10,2},{18... | collective-permute-start | bytes 786440 | tf_op jit(solution)/shard_map/ppermute | solution.py:14
  61.7 3.6 %collective-permute-start.14 = (f32[1,3,128]{2,0,1:T(1,128)S(1)}, f32[1,3,128]{2,0,1:T(1,128)S(1)}, u32[]{:S(2)}, u32[]{:S(2)}) collective-permute-start(f32[1,3,128]{2,0,1:T(1,128)S(1)} %slice_bitcast_fusion.7), channel_id=1, source_target_pairs={{6,0},{0,2},{2,4},{4,6},{7,1},{1,3},{3,5},{5,7},{14,8},{8,10},{10,... | collective-permute-start | bytes 4616 | tf_op jit(solution)/shard_map/ppermute | solution.py:14
  67.4 5.0 %collective-permute-start.10 = (f32[1,128,128]{2,1,0:T(8,128)S(1)}, f32[1,128,128]{2,1,0:T(8,128)S(1)}, u32[]{:S(2)}, u32[]{:S(2)}) collective-permute-start(f32[1,128,128]{2,1,0:T(8,128)S(1)} %slice_bitcast_fusion.3), channel_id=1, source_target_pairs={{6,0},{0,2},{2,4},{4,6},{7,1},{1,3},{3,5},{5,7},{14,8},{8,10},{10,... | collective-permute-start | bytes 196616 | tf_op jit(solution)/shard_map/ppermute | solution.py:14
  69.0 6.2 %collective-permute-start.15 = (f32[1,3,128]{2,0,1:T(1,128)S(1)}, f32[1,3,128]{2,0,1:T(1,128)S(1)}, u32[]{:S(2)}, u32[]{:S(2)}) collective-permute-start(f32[1,3,128]{2,0,1:T(1,128)S(1)} %slice_bitcast_fusion.6), channel_id=1, source_target_pairs={{2,0},{4,2},{6,4},{0,6},{3,1},{5,3},{7,5},{1,7},{10,8},{12,10},{14... | collective-permute-start | bytes 4616 | tf_op jit(solution)/shard_map/ppermute | solution.py:14
  72.5 4.6 %collective-permute-start.11 = (f32[1,128,128]{2,1,0:T(8,128)S(1)}, f32[1,128,128]{2,1,0:T(8,128)S(1)}, u32[]{:S(2)}, u32[]{:S(2)}) collective-permute-start(f32[1,128,128]{2,1,0:T(8,128)S(1)} %slice_bitcast_fusion.2), channel_id=1, source_target_pairs={{2,0},{4,2},{6,4},{0,6},{3,1},{5,3},{7,5},{1,7},{10,8},{12,10},{14... | collective-permute-start | bytes 196616 | tf_op jit(solution)/shard_map/ppermute | solution.py:14
  77.1 0.9 copy-start.4
  77.1 0.9 copy-start.6
  173.0 1.6 copy-start.7
  (6 other events, 4.4 us)
Sparse Core Ops, SparseCore 0:
  78.9 94.0 all-reduce.5
where the time goes:
time: 183 us; the launch traced here: 182 us
  blocking collectives  58.6 us (32%)
  waiting for transfers between devices  50.5 us (28%)
  matrix products  22.2 us (12%)
  starting transfers between devices  17.3 us (9%)
  between operations  15 us (8%)
  local copies, waits for them, and re-layouts  10.5 us (6%)
  other arithmetic  7.96 us (4%)
    psum x1, blocking collectives, on_device(): lax.psum((grad_wvalue, grad_wradial, grad_gain, grad_wout), ('gx', 'gy'))  58.6 us
    psum x1, waiting for transfers between devices, on_device(): lax.psum((grad_wvalue, grad_wradial, grad_gain, grad_wout), ('gx', 'gy'))  35.2 us
    ppermute x8, starting transfers between devices, passed_along(): return lax.ppermute(block, axis, route)  9.53 us
    ppermute x8, waiting for transfers between devices, passed_along(): return lax.ppermute(block, axis, route)  8.55 us
    dot_general x9, matrix products, on_device(): jnp.einsum('abkij,abkic->abjc', weights, scaled, preferred_element_type=j...  8.02 us
    dot_general x9, matrix products, on_device(): jnp.einsum('abkic,abjc->abkij', scaled, near_cells(val_ext, shift_x, shif...  5.84 us
    unnamed x28, local copies, waits for them, and re-layouts  4.4 us
    ppermute x4, starting transfers between devices, with_halo(): lax.ppermute(lax.slice_in_dim(block, 0, width, axis=dim), axis, backward)  4.36 us
  transfers between devices with their start and end apart: 17, of which 10 were waited for; matrix products, arithmetic and copies ran while one was open for 4% of the time, Pallas kernels for 0%

commit v1 on v0

--- a/solution.py
+++ b/solution.py
@@ -184,7 +184,10 @@
     ).astype(jnp.bfloat16)
     grad_wvalue = jnp.dot(flat_feat.T, grad_half, preferred_element_type=jnp.float32)
     grad_gain = jnp.dot(onehot.T, flat_carried * projected, precision=lax.Precision.HIGHEST)
-    summed_grads = lax.psum((grad_wvalue, grad_wradial, grad_gain, grad_wout), ("gx", "gy"))
+    pack_the_sample = lambda point: jax.lax.psum(
+        jax.lax.psum(point, axis_name="gy"), axis_name="gx"
+    )
+    summed_grads = pack_the_sample((grad_wvalue, grad_wradial, grad_gain, grad_wout))
     return (
         out_feat.reshape(row_count, col_count, slot_count, channels),
         grad_feat.reshape(row_count, col_count, slot_count, channels),

time: 183 us -> 161 us (0.88)
  blocking collectives: 58.6 us -> 24.8 us
  waiting for transfers between devices: 50.5 us -> 60.3 us
    psum x1 -> x2, blocking collectives: 58.6 us -> 24.8 us  [the longest x1 14.1 us: on_device(): jax.lax.psum(point, axis_name='gy')]
    psum x1 -> x2, waiting for transfers between devices: 35.2 us -> 45 us  [the longest x1 36.1 us: on_device(): jax.lax.psum(point, axis_name='gy')]
  transfers between devices with their start and end apart: 17 -> 18, of which waited for: 10 -> 11; matrix products, arithmetic and copies ran while one was open for 4% -> 5% of each run, Pallas kernels for 0% -> 0%
where the time goes in v1:
time: 161 us; the launch traced here: 159 us
  waiting for transfers between devices  60.3 us (37%)
  blocking collectives  24.8 us (15%)
  matrix products  22.2 us (14%)
  starting transfers between devices  17.3 us (11%)
  between operations  15 us (9%)
  local copies, waits for them, and re-layouts  11.3 us (7%)
  other arithmetic  7.96 us (5%)
    psum x1, waiting for transfers between devices, on_device(): jax.lax.psum(point, axis_name='gy')  36.1 us
    psum x1, blocking collectives, on_device(): jax.lax.psum(point, axis_name='gy')  14.1 us
    psum x1, blocking collectives, on_device(): jax.lax.psum(jax.lax.psum(point, axis_name='gy'), axis_name='gx')  10.7 us
    ppermute x8, starting transfers between devices, passed_along(): return lax.ppermute(block, axis, route)  9.53 us
    psum x1, waiting for transfers between devices, on_device(): jax.lax.psum(jax.lax.psum(point, axis_name='gy'), axis_name='gx')  8.93 us
    ppermute x8, waiting for transfers between devices, passed_along(): return lax.ppermute(block, axis, route)  8.55 us
    dot_general x9, matrix products, on_device(): jnp.einsum('abkij,abkic->abjc', weights, scaled, preferred_element_type=j...  8.02 us
    dot_general x9, matrix products, on_device(): jnp.einsum('abkic,abjc->abkij', scaled, near_cells(val_ext, shift_x, shif...  5.84 us
  transfers between devices with their start and end apart: 18, of which 11 were waited for; matrix products, arithmetic and copies ran while one was open for 5% of the time, Pallas kernels for 0%

profile of v1, /device:TPU:8, one launch (start us, length us, event | category | flops | bytes accessed | tf_op | source)
XLA Modules:
  0.0 158.8 jit_solution(13378939690482541474)
XLA Ops:
  8.0 1.7 %collective-permute-start.1 = (f32[1,2,4,128]{3,1,2,0:T(2,128)S(1)}, f32[1,2,4,128]{3,1,2,0:T(2,128)S(1)}, u32[]{:S(2)}, u32[]{:S(2)}) collective-permute-start(f32[1,2,4,128]{3,1,2,0:T(2,128)S(1)} %pad_maximum_fusion.8), channel_id=1, source_target_pairs={{8,0},{16,8},{24,16},{0,24},{9,1},{17,9},{25,17},{1,25},{10,2},{18... | collective-permute-start | bytes 12296 | tf_op jit(solution)/shard_map/ppermute | solution.py:26
  10.8 1.7 %collective-permute-start.4 = (bf16[1,2,128,128]{3,2,1,0:T(8,128)(2,1)S(1)}, bf16[1,2,128,128]{3,2,1,0:T(8,128)(2,1)S(1)}, u32[]{:S(2)}, u32[]{:S(2)}) collective-permute-start(bf16[1,2,128,128]{3,2,1,0:T(8,128)(2,1)S(1)} %bitcast.389), channel_id=1, source_target_pairs={{8,0},{16,8},{24,16},{0,24},{9,1},{17,9},{25,17},{1,25},{10,2},{18... | collective-permute-start | bytes 196616 | tf_op jit(solution)/shard_map/ppermute | solution.py:26
  14.6 1.6 %collective-permute-start.2 = (f32[3,1,4,128]{3,1,2,0:T(1,128)S(1)}, f32[3,1,4,128]{3,1,2,0:T(1,128)S(1)}, u32[]{:S(2)}, u32[]{:S(2)}) collective-permute-start(f32[3,1,4,128]{3,1,2,0:T(1,128)S(1)} %get-tuple-element.620), channel_id=1, source_target_pairs={{0,2},{2,4},{4,6},{6,0},{1,3},{3,5},{5,7},{7,1},{8,10},{10,12},{12... | collective-permute-start | bytes 18440 | tf_op jit(solution)/shard_map/ppermute | solution.py:23
  16.7 1.6 %collective-permute-done.2 = f32[3,1,4,128]{3,1,2,0:T(1,128)S(1)} collective-permute-done((f32[3,1,4,128]{3,1,2,0:T(1,128)S(1)}, f32[3,1,4,128]{3,1,2,0:T(1,128)S(1)}, u32[]{:S(2)}, u32[]{:S(2)}) %collective-permute-start.2) | collective-permute-done | bytes 6176 | tf_op jit(solution)/shard_map/ppermute | solution.py:23
  18.4 1.5 collective-permute-done.6
  21.9 1.6 %collective-permute-start.5 = (bf16[3,1,128,128]{3,2,1,0:T(8,128)(2,1)S(1)}, bf16[3,1,128,128]{3,2,1,0:T(8,128)(2,1)S(1)}, u32[]{:S(2)}, u32[]{:S(2)}) collective-permute-start(bf16[3,1,128,128]{3,2,1,0:T(8,128)(2,1)S(1)} %get-tuple-element.586), channel_id=1, source_target_pairs={{0,2},{2,4},{4,6},{6,0},{1,3},{3,5},{5,7},{7,1},{8,10},{10,12},{12... | collective-permute-start | bytes 294920 | tf_op jit(solution)/shard_map/ppermute | solution.py:23
  24.8 2.5 %collective-permute-done.5 = bf16[3,1,128,128]{3,2,1,0:T(8,128)(2,1)S(1)} collective-permute-done((bf16[3,1,128,128]{3,2,1,0:T(8,128)(2,1)S(1)}, bf16[3,1,128,128]{3,2,1,0:T(8,128)(2,1)S(1)}, u32[]{:S(2)}, u32[]{:S(2)}) %collective-permute-start.5) | collective-permute-done | bytes 98336 | tf_op jit(solution)/shard_map/ppermute | solution.py:23
  33.9 1.8 %fusion.16 = f32[3,4,128,128]{3,2,1,0:T(8,128)S(1)} fusion(f32[3,4,128,128]{3,2,1,0:T(8,128)S(1)} %scatter-add.104, s32[]{:T(128)} %bitcast.74, s32[]{:T(128)} %bitcast.75, f32[2,128,128]{2,1,0:T(8,128)S(1)} %bitcast_convert_fusion, f32[8,128]{1,0:T(8,128)S(1)} %copy-done.9, f32[2,128,128]{2,1,0:T(8,128)S(1)} %get-tuple-element.670, ...), kind=kOutput, calls=%fused_computation.63 | convolution fusion | flops 68976640 | bytes 659976 | tf_op jit(solution)/shard_map/abkij,abkic->abjc/dot_general | solution.py:168
  35.8 2.5 %fusion.19 = f32[3,4,128,128]{3,2,1,0:T(8,128)S(1)} fusion(f32[3,4,128,128]{3,2,1,0:T(8,128)S(1)} %fusion.16, s32[]{:T(128)} %bitcast.79, s32[]{:T(128)} %bitcast.80, f32[2,128,128]{2,1,0:T(8,128)S(1)} %bitcast_convert_fusion, f32[8,128]{1,0:T(8,128)S(1)} %copy-done.9, f32[2,128,128]{2,1,0:T(8,128)S(1)} %get-tuple-element.657, ...), kind=kOutput, calls=%fused_computation.66 | convolution fusion | flops 69009408 | bytes 659977 | tf_op jit(solution)/shard_map/abkij,abkic->abjc/dot_general | solution.py:168
  50.8 1.4 scatter-add.126
  52.4 2.0 %add_select_fusion = f32[1,2,3,128]{3,1,2,0:T(2,128)S(1)} fusion(f32[3,4,3,128]{3,1,2,0:T(4,128)S(1)} %scatter-add.129, s32[]{:T(128)} %bitcast.79, s32[]{:T(128)} %bitcast.80, f32[1,2,1,128]{3,1,2,0:T(2,128)S(1)} %get-tuple-element.730, f32[1,2,1,128]{3,1,2,0:T(2,128)S(1)} %get-tuple-element.731, f32[1,2,1,128]{3,1,2,0:T(2,128)S(1)} %get-tuple-element.732, ...), kind=kLoop, calls=%fused_computation.451 | loop fusion | flops 3072 | bytes 9225 | tf_op jit(solution)/shard_map/select.53
  54.4 1.4 scatter-add.130
  57.3 1.7 %collective-permute-start.13 = (f32[4,3,128]{2,0,1:T(4,128)S(1)}, f32[4,3,128]{2,0,1:T(4,128)S(1)}, u32[]{:S(2)}, u32[]{:S(2)}) collective-permute-start(f32[4,3,128]{2,0,1:T(4,128)S(1)} %get-tuple-element.595), channel_id=1, source_target_pairs={{8,0},{16,8},{24,16},{0,24},{9,1},{17,9},{25,17},{1,25},{10,2},{18... | collective-permute-start | bytes 18440 | tf_op jit(solution)/shard_map/ppermute | solution.py:14
  59.9 1.7 %collective-permute-start.9 = (f32[4,128,128]{2,1,0:T(8,128)S(1)}, f32[4,128,128]{2,1,0:T(8,128)S(1)}, u32[]{:S(2)}, u32[]{:S(2)}) collective-permute-start(f32[4,128,128]{2,1,0:T(8,128)S(1)} %get-tuple-element.579), channel_id=1, source_target_pairs={{8,0},{16,8},{24,16},{0,24},{9,1},{17,9},{25,17},{1,25},{10,2},{18... | collective-permute-start | bytes 786440 | tf_op jit(solution)/shard_map/ppermute | solution.py:14
  63.0 2.3 %collective-permute-done.14 = f32[1,3,128]{2,0,1:T(1,128)S(1)} collective-permute-done((f32[1,3,128]{2,0,1:T(1,128)S(1)}, f32[1,3,128]{2,0,1:T(1,128)S(1)}, u32[]{:S(2)}, u32[]{:S(2)}) %collective-permute-start.14) | collective-permute-done | bytes 1568 | tf_op jit(solution)/shard_map/ppermute | solution.py:14
  65.3 1.5 collective-permute-done.8
  67.4 1.5 collective-permute-start.10
  69.5 2.9 %collective-permute-done.10 = f32[1,128,128]{2,1,0:T(8,128)S(1)} collective-permute-done((f32[1,128,128]{2,1,0:T(8,128)S(1)}, f32[1,128,128]{2,1,0:T(8,128)S(1)}, u32[]{:S(2)}, u32[]{:S(2)}) %collective-permute-start.10) | collective-permute-done | bytes 65568 | tf_op jit(solution)/shard_map/ppermute | solution.py:14
  72.5 2.7 %collective-permute-start.11 = (f32[1,128,128]{2,1,0:T(8,128)S(1)}, f32[1,128,128]{2,1,0:T(8,128)S(1)}, u32[]{:S(2)}, u32[]{:S(2)}) collective-permute-start(f32[1,128,128]{2,1,0:T(8,128)S(1)} %slice_bitcast_fusion.2), channel_id=1, source_target_pairs={{2,0},{4,2},{6,4},{0,6},{3,1},{5,3},{7,5},{1,7},{10,8},{12,10},{14... | collective-permute-start | bytes 196616 | tf_op jit(solution)/shard_map/ppermute | solution.py:14
  79.6 36.1 %all-reduce.9.cloned.1.call-done = (f32[128,128]{0,1:T(8,128)}, f32[128,128]{1,0:T(8,128)}) async-done(((f32[128,128]{0,1:T(8,128)}, f32[128,128]{1,0:T(8,128)}), (f32[128,128]{0,1:T(8,128)}, f32[128,128]{1,0:T(8,128)})) %all-reduce.9.cloned.1.call-update) | async-done | bytes 131088 | tf_op jit(solution)/shard_map/psum | solution.py:188
  116.0 14.1 %all-reduce.2 = (f32[8,128]{1,0:T(8,128)S(1)}, f32[16,128]{1,0:T(8,128)S(1)}) all-reduce(f32[8,128]{1,0:T(8,128)S(1)} %multiply_reduce_fusion, f32[16,128]{1,0:T(8,128)S(1)} %fusion.203), channel_id=1, replica_groups=mesh['gx'=4,'gy'=4,'frame'=2] {'gy'}, use_global_device_ids=true, to_apply=%region_68.0 | all-reduce | flops 3072 | bytes 24576 | tf_op jit(solution)/shard_map/psum | solution.py:188
  130.1 10.7 %all-reduce.4 = (f32[8,128]{1,0:T(8,128)}, f32[16,128]{1,0:T(8,128)}) all-reduce(f32[8,128]{1,0:T(8,128)S(1)} %get-tuple-element.567, f32[16,128]{1,0:T(8,128)S(1)} %get-tuple-element.568), channel_id=1, replica_groups=mesh['gx'=4,'gy'=4,'frame'=2] {'gx'}, use_global_device_ids=true, to_apply=%region_69.0 | all-reduce | flops 3072 | bytes 24576 | tf_op jit(solution)/shard_map/psum | solution.py:187
  140.8 8.9 %all-reduce.11.cloned.1.call-done = (f32[128,128]{0,1:T(8,128)}, f32[128,128]{1,0:T(8,128)}) async-done(((f32[128,128]{0,1:T(8,128)}, f32[128,128]{1,0:T(8,128)}), (f32[128,128]{0,1:T(8,128)}, f32[128,128]{1,0:T(8,128)})) %all-reduce.11.cloned.1.call-update) | async-done | bytes 131088 | tf_op jit(solution)/shard_map/psum | solution.py:187
  149.8 1.6 %copy.44 = f32[128,128]{1,0:T(8,128)} copy(f32[128,128]{0,1:T(8,128)} %get-tuple-element.573) | data formatting | bytes 131072
  (183 shorter events, 36.6 us)
Async XLA Ops:
  7.2 24.9 %copy-start = (bf16[128,128]{1,0:T(8,128)(2,1)S(1)}, bf16[128,128]{1,0:T(8,128)(2,1)}, u32[]{:S(2)}) copy-start(bf16[128,128]{1,0:T(8,128)(2,1)} %param.86) | copy-start | bytes 98308
  7.2 2.5 %copy-start.8 = (f32[16,128]{1,0:T(8,128)S(1)}, f32[16,128]{1,0:T(8,128)}, u32[]{:S(2)}) copy-start(f32[16,128]{1,0:T(8,128)} %param.85) | copy-start | bytes 24580
  7.2 108.5 %all-reduce.9.cloned.1.call-start = ((), (), s32[]{:S(2)}) async-start(), calls=%async_computation | async-start | bytes 262144 | tf_op jit(solution)/shard_map/psum | solution.py:188
  7.9 1.8 %copy-start.10 = (s32[1,2,128]{2,1,0:T(2,128)S(1)}, s32[1,2,128]{2,1,0:T(2,128)}, u32[]{:S(2)}) copy-start(s32[1,2,128]{2,1,0:T(2,128)} %param.81) | copy-start | bytes 3076
  7.9 6.7 %collective-permute-start = (f32[1,2,4,128]{3,1,2,0:T(2,128)S(1)}, f32[1,2,4,128]{3,1,2,0:T(2,128)S(1)}, u32[]{:S(2)}, u32[]{:S(2)}) collective-permute-start(f32[1,2,4,128]{3,1,2,0:T(2,128)S(1)} %pad_maximum_fusion.8), channel_id=1, source_target_pairs={{0,8},{8,16},{16,24},{24,0},{1,9},{9,17},{17,25},{25,1},{2,10},{10... | collective-permute-start | bytes 12296 | tf_op jit(solution)/shard_map/ppermute | solution.py:23
  8.0 6.6 %collective-permute-start.1 = (f32[1,2,4,128]{3,1,2,0:T(2,128)S(1)}, f32[1,2,4,128]{3,1,2,0:T(2,128)S(1)}, u32[]{:S(2)}, u32[]{:S(2)}) collective-permute-start(f32[1,2,4,128]{3,1,2,0:T(2,128)S(1)} %pad_maximum_fusion.8), channel_id=1, source_target_pairs={{8,0},{16,8},{24,16},{0,24},{9,1},{17,9},{25,17},{1,25},{10,2},{18... | collective-permute-start | bytes 12296 | tf_op jit(solution)/shard_map/ppermute | solution.py:26
  9.7 0.8 copy-start.3
  10.7 11.1 %collective-permute-start.3 = (bf16[1,2,128,128]{3,2,1,0:T(8,128)(2,1)S(1)}, bf16[1,2,128,128]{3,2,1,0:T(8,128)(2,1)S(1)}, u32[]{:S(2)}, u32[]{:S(2)}) collective-permute-start(bf16[1,2,128,128]{3,2,1,0:T(8,128)(2,1)S(1)} %bitcast.388), channel_id=1, source_target_pairs={{0,8},{8,16},{16,24},{24,0},{1,9},{9,17},{17,25},{25,1},{2,10},{10... | collective-permute-start | bytes 196616 | tf_op jit(solution)/shard_map/ppermute | solution.py:23
  10.8 11.0 %collective-permute-start.4 = (bf16[1,2,128,128]{3,2,1,0:T(8,128)(2,1)S(1)}, bf16[1,2,128,128]{3,2,1,0:T(8,128)(2,1)S(1)}, u32[]{:S(2)}, u32[]{:S(2)}) collective-permute-start(bf16[1,2,128,128]{3,2,1,0:T(8,128)(2,1)S(1)} %bitcast.389), channel_id=1, source_target_pairs={{8,0},{16,8},{24,16},{0,24},{9,1},{17,9},{25,17},{1,25},{10,2},{18... | collective-permute-start | bytes 196616 | tf_op jit(solution)/shard_map/ppermute | solution.py:26
  14.6 3.7 %collective-permute-start.2 = (f32[3,1,4,128]{3,1,2,0:T(1,128)S(1)}, f32[3,1,4,128]{3,1,2,0:T(1,128)S(1)}, u32[]{:S(2)}, u32[]{:S(2)}) collective-permute-start(f32[3,1,4,128]{3,1,2,0:T(1,128)S(1)} %get-tuple-element.620), channel_id=1, source_target_pairs={{0,2},{2,4},{4,6},{6,0},{1,3},{3,5},{5,7},{7,1},{8,10},{10,12},{12... | collective-permute-start | bytes 18440 | tf_op jit(solution)/shard_map/ppermute | solution.py:23
  16.3 3.6 %collective-permute-start.6 = (f32[3,1,4,128]{3,1,2,0:T(1,128)S(1)}, f32[3,1,4,128]{3,1,2,0:T(1,128)S(1)}, u32[]{:S(2)}, u32[]{:S(2)}) collective-permute-start(f32[3,1,4,128]{3,1,2,0:T(1,128)S(1)} %get-tuple-element.621), channel_id=1, source_target_pairs={{2,0},{4,2},{6,4},{0,6},{3,1},{5,3},{7,5},{1,7},{10,8},{12,10},{14... | collective-permute-start | bytes 18440 | tf_op jit(solution)/shard_map/ppermute | solution.py:26
  21.9 5.4 %collective-permute-start.5 = (bf16[3,1,128,128]{3,2,1,0:T(8,128)(2,1)S(1)}, bf16[3,1,128,128]{3,2,1,0:T(8,128)(2,1)S(1)}, u32[]{:S(2)}, u32[]{:S(2)}) collective-permute-start(bf16[3,1,128,128]{3,2,1,0:T(8,128)(2,1)S(1)} %get-tuple-element.586), channel_id=1, source_target_pairs={{0,2},{2,4},{4,6},{6,0},{1,3},{3,5},{5,7},{7,1},{8,10},{10,12},{12... | collective-permute-start | bytes 294920 | tf_op jit(solution)/shard_map/ppermute | solution.py:23
  23.5 5.3 %collective-permute-start.7 = (bf16[3,1,128,128]{3,2,1,0:T(8,128)(2,1)S(1)}, bf16[3,1,128,128]{3,2,1,0:T(8,128)(2,1)S(1)}, u32[]{:S(2)}, u32[]{:S(2)}) collective-permute-start(bf16[3,1,128,128]{3,2,1,0:T(8,128)(2,1)S(1)} %get-tuple-element.587), channel_id=1, source_target_pairs={{2,0},{4,2},{6,4},{0,6},{3,1},{5,3},{7,5},{1,7},{10,8},{12,10},{14... | collective-permute-start | bytes 294920 | tf_op jit(solution)/shard_map/ppermute | solution.py:26
  57.3 4.4 %collective-permute-start.12 = (f32[4,3,128]{2,0,1:T(4,128)S(1)}, f32[4,3,128]{2,0,1:T(4,128)S(1)}, u32[]{:S(2)}, u32[]{:S(2)}) collective-permute-start(f32[4,3,128]{2,0,1:T(4,128)S(1)} %get-tuple-element.594), channel_id=1, source_target_pairs={{24,0},{0,8},{8,16},{16,24},{25,1},{1,9},{9,17},{17,25},{26,2},{2,... | collective-permute-start | bytes 18440 | tf_op jit(solution)/shard_map/ppermute | solution.py:14
  57.3 4.3 %collective-permute-start.13 = (f32[4,3,128]{2,0,1:T(4,128)S(1)}, f32[4,3,128]{2,0,1:T(4,128)S(1)}, u32[]{:S(2)}, u32[]{:S(2)}) collective-permute-start(f32[4,3,128]{2,0,1:T(4,128)S(1)} %get-tuple-element.595), channel_id=1, source_target_pairs={{8,0},{16,8},{24,16},{0,24},{9,1},{17,9},{25,17},{1,25},{10,2},{18... | collective-permute-start | bytes 18440 | tf_op jit(solution)/shard_map/ppermute | solution.py:14
  59.9 6.9 %collective-permute-start.8 = (f32[4,128,128]{2,1,0:T(8,128)S(1)}, f32[4,128,128]{2,1,0:T(8,128)S(1)}, u32[]{:S(2)}, u32[]{:S(2)}) collective-permute-start(f32[4,128,128]{2,1,0:T(8,128)S(1)} %get-tuple-element.578), channel_id=1, source_target_pairs={{24,0},{0,8},{8,16},{16,24},{25,1},{1,9},{9,17},{17,25},{26,2},{2,... | collective-permute-start | bytes 786440 | tf_op jit(solution)/shard_map/ppermute | solution.py:14
  59.9 7.5 %collective-permute-start.9 = (f32[4,128,128]{2,1,0:T(8,128)S(1)}, f32[4,128,128]{2,1,0:T(8,128)S(1)}, u32[]{:S(2)}, u32[]{:S(2)}) collective-permute-start(f32[4,128,128]{2,1,0:T(8,128)S(1)} %get-tuple-element.579), channel_id=1, source_target_pairs={{8,0},{16,8},{24,16},{0,24},{9,1},{17,9},{25,17},{1,25},{10,2},{18... | collective-permute-start | bytes 786440 | tf_op jit(solution)/shard_map/ppermute | solution.py:14
  61.7 3.6 %collective-permute-start.14 = (f32[1,3,128]{2,0,1:T(1,128)S(1)}, f32[1,3,128]{2,0,1:T(1,128)S(1)}, u32[]{:S(2)}, u32[]{:S(2)}) collective-permute-start(f32[1,3,128]{2,0,1:T(1,128)S(1)} %slice_bitcast_fusion.7), channel_id=1, source_target_pairs={{6,0},{0,2},{2,4},{4,6},{7,1},{1,3},{3,5},{5,7},{14,8},{8,10},{10,... | collective-permute-start | bytes 4616 | tf_op jit(solution)/shard_map/ppermute | solution.py:14
  67.4 5.0 %collective-permute-start.10 = (f32[1,128,128]{2,1,0:T(8,128)S(1)}, f32[1,128,128]{2,1,0:T(8,128)S(1)}, u32[]{:S(2)}, u32[]{:S(2)}) collective-permute-start(f32[1,128,128]{2,1,0:T(8,128)S(1)} %slice_bitcast_fusion.3), channel_id=1, source_target_pairs={{6,0},{0,2},{2,4},{4,6},{7,1},{1,3},{3,5},{5,7},{14,8},{8,10},{10,... | collective-permute-start | bytes 196616 | tf_op jit(solution)/shard_map/ppermute | solution.py:14
  69.0 6.2 %collective-permute-start.15 = (f32[1,3,128]{2,0,1:T(1,128)S(1)}, f32[1,3,128]{2,0,1:T(1,128)S(1)}, u32[]{:S(2)}, u32[]{:S(2)}) collective-permute-start(f32[1,3,128]{2,0,1:T(1,128)S(1)} %slice_bitcast_fusion.6), channel_id=1, source_target_pairs={{2,0},{4,2},{6,4},{0,6},{3,1},{5,3},{7,5},{1,7},{10,8},{12,10},{14... | collective-permute-start | bytes 4616 | tf_op jit(solution)/shard_map/ppermute | solution.py:14
  72.5 4.6 %collective-permute-start.11 = (f32[1,128,128]{2,1,0:T(8,128)S(1)}, f32[1,128,128]{2,1,0:T(8,128)S(1)}, u32[]{:S(2)}, u32[]{:S(2)}) collective-permute-start(f32[1,128,128]{2,1,0:T(8,128)S(1)} %slice_bitcast_fusion.2), channel_id=1, source_target_pairs={{2,0},{4,2},{6,4},{0,6},{3,1},{5,3},{7,5},{1,7},{10,8},{12,10},{14... | collective-permute-start | bytes 196616 | tf_op jit(solution)/shard_map/ppermute | solution.py:14
  78.0 0.9 copy-start.6
  78.0 71.8 %all-reduce.11.cloned.1.call-start = ((), (), s32[]{:S(2)}) async-start(), calls=%async_computation.1 | async-start | bytes 262144 | tf_op jit(solution)/shard_map/psum | solution.py:187
  149.8 1.6 %copy-start.7 = (f32[128,128]{1,0:T(8,128)S(1)}, f32[128,128]{1,0:T(8,128)}, u32[]{:S(2)}) copy-start(f32[128,128]{1,0:T(8,128)} %get-tuple-element.766) | copy-start | bytes 196612
  (7 other events, 5.2 us)
Sparse Core Ops, SparseCore 0:
  78.1 37.5 all-reduce.8
  118.1 31.6 all-reduce.10
